TPU v7x, 32 devices: a whole 2x2x4 slice. The times are simulated.
32 devices in a mesh: inner: 4 (over y, x), blk: 8 (over z, core).
Axes of the slice: x: 2, y: 2, z: 4, core: 2. Of those that a mesh axis runs over, the one named last changes fastest.
Arguments:
- image_emb: float32 [768, 768], P(('inner', 'blk')), may hold values from -150 to 150
- text_emb: float32 [768, 768], P(('inner', 'blk')), may hold values from -150 to 150
- logit_scale: float32 [1], replicated, may hold values from 30 to 100
Outputs:
- mean_loss: float32 [1], replicated
- image_grad: float32 [768, 768], P(('inner', 'blk'))
- text_grad: float32 [768, 768], P(('inner', 'blk'))
All inputs are finite; a program needn't handle non-finite values.
Results may differ from a plain program's by a relative error of at most 0.006.
Values may be sent and summed in bfloat16 or wider, within the bound.
A program may use at most 64 MiB of HBM per device.

v0:
```python
import jax
import jax.numpy as jnp
from jax import lax
from jax.sharding import PartitionSpec as P

EPSILON = 1e-06


def unit_rows(values):
    inverse = lax.rsqrt(jnp.sum(values * values, axis=1, keepdims=True) + EPSILON)
    return (values * inverse, inverse)


def project(gradient, direction, inverse):
    return (gradient - direction * jnp.sum(gradient * direction, axis=1, keepdims=True)) * inverse


def gather_rows(values, wide_axis):
    if wide_axis:
        return lax.all_gather(values, "blk", axis=0, tiled=True)
    return lax.all_gather(values, "inner", axis=0, tiled=True)


def merge_stats(peaks, totals, wide_axis):
    if wide_axis:
        highest = lax.pmax(peaks, "blk")
    else:
        highest = lax.pmax(peaks, "inner")
    scaled = totals * jnp.exp(peaks - highest)
    if wide_axis:
        scaled = lax.psum(scaled, "blk")
    else:
        scaled = lax.psum(scaled, "inner")
    return highest + jnp.log(scaled)


def reduce_rows(partial_value, wide_axis):
    if wide_axis:
        return lax.psum_scatter(partial_value, "blk", scatter_dimension=0, tiled=True)
    return lax.psum_scatter(partial_value, "inner", scatter_dimension=0, tiled=True)


def own_index(wide_axis):
    if wide_axis:
        return lax.axis_index("blk")
    return lax.axis_index("inner")


def on_device(image_emb, text_emb, logit_scale):
    own_rows, embed_width = image_emb.shape
    factor = logit_scale[0]
    image_unit, image_inverse = unit_rows(image_emb)
    text_unit, text_inverse = unit_rows(text_emb)
    image_half = image_unit.astype(jnp.bfloat16)
    text_half = text_unit.astype(jnp.bfloat16)
    image_group = gather_rows(image_half, False)
    text_group = gather_rows(text_half, True)
    image_count = image_group.shape[0]
    text_count = text_group.shape[0]
    pieces = max(1, text_count // 128)
    text_blocks = text_group.reshape(pieces, text_count // pieces, embed_width)
    contract_last = (((1,), (1,)), ((), ()))
    contract_first = (((0,), (0,)), ((), ()))

    def scores(text_block):
        return factor * lax.dot_general(
            image_group, text_block, contract_last, preferred_element_type=jnp.float32
        )

    def first_pass(state, text_block):
        row_peak, row_total = state
        logits = scores(text_block)
        new_peak = jnp.maximum(row_peak, jnp.max(logits, axis=1))
        row_total = row_total * jnp.exp(row_peak - new_peak) + jnp.sum(
            jnp.exp(logits - new_peak[:, None]), axis=1
        )
        col_peak = jnp.max(logits, axis=0)
        col_total = jnp.sum(jnp.exp(logits - col_peak[None, :]), axis=0)
        return ((new_peak, row_total), (col_peak, col_total))

    initial = (jnp.full((image_count,), -1e30, jnp.float32), jnp.zeros((image_count,), jnp.float32))
    (row_peak, row_total), (col_peak, col_total) = lax.scan(first_pass, initial, text_blocks)
    row_lse = merge_stats(row_peak, row_total, False)
    col_lse = merge_stats(col_peak.reshape(text_count), col_total.reshape(text_count), True)
    half_factor = 0.5 * factor

    def make_weights(text_block, col_block):
        logits = scores(text_block)
        return (
            half_factor
            * (jnp.exp(logits - row_lse[:, None]) + jnp.exp(logits - col_block[None, :]))
        ).astype(jnp.bfloat16)

    col_blocks = col_lse.reshape(pieces, text_count // pieces)
    empty = jnp.zeros((image_count, embed_width), jnp.float32)

    def second_pass(image_acc, inputs):
        text_block, col_block = inputs
        weights = make_weights(text_block, col_block)
        image_acc = image_acc + jnp.dot(weights, text_block, preferred_element_type=jnp.float32)
        text_part = lax.dot_general(
            weights, image_group, contract_first, preferred_element_type=jnp.float32
        )
        return (image_acc, text_part)

    image_partial, text_parts = lax.scan(second_pass, empty, (text_blocks, col_blocks))
    text_sum = reduce_rows(text_parts.reshape(text_count, embed_width), True)
    image_sum = reduce_rows(image_partial, False)
    diagonal = factor * jnp.sum(
        image_half.astype(jnp.float32) * text_half.astype(jnp.float32), axis=1
    )
    row_own = lax.dynamic_slice_in_dim(row_lse, own_index(False) * own_rows, own_rows)
    col_own = lax.dynamic_slice_in_dim(col_lse, own_index(True) * own_rows, own_rows)
    share = jnp.sum(row_own - diagonal) + jnp.sum(col_own - diagonal)
    whole_count = own_rows * lax.axis_size("inner") * lax.axis_size("blk")
    mean_loss = (lax.psum(share, ("inner", "blk")) / (2.0 * whole_count)).reshape(1)
    image_pull = image_sum - factor * text_half.astype(jnp.float32)
    text_pull = text_sum - factor * image_half.astype(jnp.float32)
    image_grad = project(image_pull, image_unit, image_inverse)
    text_grad = project(text_pull, text_unit, text_inverse)
    return (mean_loss, image_grad, text_grad)


def solution(mesh):
    in_specs = (P(("inner", "blk"), None), P(("inner", "blk"), None), P())
    out_specs = (P(), P(("inner", "blk"), None), P(("inner", "blk"), None))
    return jax.shard_map(
        on_device, mesh=mesh, in_specs=in_specs, out_specs=out_specs, check_vma=False
    )
```

profile of v0, /device:TPU:0, one launch (start us, length us, event | category | flops | bytes accessed | tf_op | source)
XLA Modules:
  0.0 186.4 jit_solution(16345428228453393818)
XLA Ops:
  7.2 0.0 copy-start.1
  7.2 0.0 reduce-scatter.7.cloned.1.call-start
  7.9 1.0 multiply_reduce_fusion.2
  8.9 0.0 copy-done.1
  8.9 0.1 multiply_convert_fusion.1
  9.0 0.0 copy-start
  9.0 16.1 %all_gather.7 = bf16[192,768]{1,0:T(8,128)(2,1)S(1)} all-gather(bf16[24,768]{1,0:T(8,128)(2,1)S(1)} %multiply_convert_fusion.1), channel_id=1, replica_groups=mesh['inner'=4,'blk'=8] {'blk'}, dimensions={0}, use_global_device_ids=true | all-gather | bytes 331776 | tf_op jit(solution)/shard_map/all_gather | solution.py:20
  25.0 0.0 copy-done
  25.0 0.1 multiply_reduce_fusion.3
  25.2 0.1 multiply_convert_fusion.2
  25.2 8.6 %all_gather.6 = bf16[96,768]{1,0:T(8,128)(2,1)S(1)} all-gather(bf16[24,768]{1,0:T(8,128)(2,1)S(1)} %multiply_convert_fusion.2), channel_id=1, replica_groups=mesh['inner'=4,'blk'=8] {'inner'}, dimensions={0}, use_global_device_ids=true | all-gather | bytes 184320 | tf_op jit(solution)/shard_map/all_gather | solution.py:21
  33.8 0.3 fusion.5
  34.2 9.0 %pmax.14 = f32[96]{0:T(128)S(1)} all-reduce(f32[96]{0:T(128)S(1)} %broadcast_maximum_fusion), channel_id=1, replica_groups=mesh['inner'=4,'blk'=8] {'inner'}, use_global_device_ids=true, to_apply=%region_3.0 | all-reduce | flops 96 | bytes 768 | tf_op jit(solution)/shard_map/pmax | solution.py:28
  43.1 13.6 %pmax.15 = f32[192]{0:T(256)S(1)} all-reduce(f32[192]{0:T(256)S(1)} %get-tuple-element.38), channel_id=1, replica_groups=mesh['inner'=4,'blk'=8] {'blk'}, use_global_device_ids=true, to_apply=%region_9.10 | all-reduce | flops 192 | bytes 1536 | tf_op jit(solution)/shard_map/pmax | solution.py:26
  56.7 0.2 exponential_reduce_fusion
  56.9 8.9 %psum.21 = f32[96]{0:T(128)S(1)} all-reduce(f32[96]{0:T(128)S(1)} %exponential_multiply_fusion.1), channel_id=1, replica_groups=mesh['inner'=4,'blk'=8] {'inner'}, use_global_device_ids=true, to_apply=%region_5.0 | all-reduce | flops 96 | bytes 768 | tf_op jit(solution)/shard_map/psum | solution.py:33
  65.8 13.6 %psum.22 = f32[192]{0:T(256)S(1)} all-reduce(f32[192]{0:T(256)S(1)} %exponential_multiply_fusion), channel_id=1, replica_groups=mesh['inner'=4,'blk'=8] {'blk'}, use_global_device_ids=true, to_apply=%region_11.12 | all-reduce | flops 192 | bytes 1536 | tf_op jit(solution)/shard_map/psum | solution.py:31
  79.4 1.0 fusion.4
  80.4 0.0 reduce-scatter.7.cloned.1.call-update
  80.4 0.0 reduce-scatter.5.cloned.1.call-start
  80.5 1.2 fusion.3
  81.6 0.0 reduce-scatter.5.cloned.1.call-update
  81.6 20.6 %reduce-scatter.7.cloned.1.call-done = f32[24,768]{1,0:T(8,128)} async-done(((f32[96,768]{1,0:T(8,128)}), f32[24,768]{1,0:T(8,128)}) %reduce-scatter.7.cloned.1.call-update) | async-done | bytes 73744
  102.2 33.8 %reduce-scatter.5.cloned.1.call-done = f32[24,768]{1,0:T(8,128)} async-done(((f32[192,768]{1,0:T(8,128)}), f32[24,768]{1,0:T(8,128)}) %reduce-scatter.5.cloned.1.call-update) | async-done | bytes 73744 | tf_op jit(solution)/shard_map/reduce_scatter | solution.py:39
  136.0 0.0 copy-start.2
  136.0 0.0 copy-start.3
  136.0 1.2 multiply_reduce_fusion
  137.2 0.7 subtract_reduce_fusion
  139.2 37.8 %psum.23 = f32[]{:T(128)} all-reduce(f32[]{:T(128)S(6)} %add.62), channel_id=1, replica_groups=mesh['inner'=4,'blk'=8] {'inner','blk'}, use_global_device_ids=true, to_apply=%region_13.14 | all-reduce | flops 1 | bytes 8 | tf_op jit(solution)/shard_map/psum | solution.py:116
  177.6 0.0 copy-done.2
  177.6 0.0 copy-done.3
  177.6 0.8 subtract_multiply_fusion
  (7 shorter events, 0.1 us)
Async XLA Ops:
  7.2 1.7 copy-start.1
  7.2 95.0 %reduce-scatter.7.cloned.1.call-start = ((), (), s32[]{:S(2)}) async-start(), calls=%async_computation.3 | async-start | bytes 368640
  9.0 16.1 %copy-start = (f32[24,768]{1,0:T(8,128)S(1)}, f32[24,768]{1,0:T(8,128)}, u32[]{:S(2)}) copy-start(f32[24,768]{1,0:T(8,128)} %param.3) | copy-start | bytes 221188
  80.4 55.6 %reduce-scatter.5.cloned.1.call-start = ((), (), s32[]{:S(2)}) async-start(), calls=%async_computation.2 | async-start | bytes 663552 | tf_op jit(solution)/shard_map/reduce_scatter | solution.py:39
  136.0 41.6 %copy-start.2 = (f32[24,768]{1,0:T(8,128)S(1)}, f32[24,768]{1,0:T(8,128)}, u32[]{:S(2)}) copy-start(f32[24,768]{1,0:T(8,128)} %reduce-scatter.7.cloned.1.call-done) | copy-start | bytes 221188
  136.0 41.6 %copy-start.3 = (f32[24,768]{1,0:T(8,128)S(1)}, f32[24,768]{1,0:T(8,128)}, u32[]{:S(2)}) copy-start(f32[24,768]{1,0:T(8,128)} %reduce-scatter.5.cloned.1.call-done) | copy-start | bytes 221188
Sparse Core Ops, SparseCore 0:
  80.5 21.6 reduce-scatter.6
  104.5 31.4 reduce-scatter.4
where the time goes:
time: 188 us; the launch traced here: 186 us
  blocking collectives  107 us (57%)
  waiting for transfers between devices  54.4 us (29%)
  between operations  17.8 us (9%)
  other arithmetic  4.15 us (2%)
  matrix products  2.46 us (1%)
    psum x1, blocking collectives, on_device(): lax.psum(share, ('inner', 'blk')) / (2.0 * whole_count)  37.8 us
    reduce_scatter x1, waiting for transfers between devices, reduce_rows(): lax.psum_scatter(partial_value, 'blk', scatter_dimension=0, tiled=True)  33.8 us
    unnamed x3, waiting for transfers between devices  20.6 us
    all_gather x1, blocking collectives, gather_rows(): return lax.all_gather(values, 'blk', axis=0, tiled=True)  16.1 us
    psum x1, blocking collectives, merge_stats(): scaled = lax.psum(scaled, 'blk')  13.6 us
    pmax x1, blocking collectives, merge_stats(): highest = lax.pmax(peaks, 'blk')  13.6 us
    pmax x1, blocking collectives, merge_stats(): highest = lax.pmax(peaks, 'inner')  8.96 us
    psum x1, blocking collectives, merge_stats(): scaled = lax.psum(scaled, 'inner')  8.88 us
  transfers between devices with their start and end apart: 2, of which 2 were waited for; matrix products, arithmetic and copies ran while one was open for 1% of the time, Pallas kernels for 0%

commit v1 on v0

v1 whole, which is shorter than its diff:
```python
import functools

import jax
import jax.numpy as jnp
from jax import lax
from jax.experimental import pallas as pl
from jax.experimental.pallas import tpu as pltpu
from jax.sharding import PartitionSpec as P

EPSILON = 1e-06
MESH = pl.DeviceIdType.MESH


def unit_rows(values):
    inverse = lax.rsqrt(jnp.sum(values * values, axis=1, keepdims=True) + EPSILON)
    return (values * inverse, inverse)


def project(gradient, direction, inverse):
    return (gradient - direction * jnp.sum(gradient * direction, axis=1, keepdims=True)) * inverse


class Group:
    def __init__(self, me, size, device_of, sems):
        self.me, self.size, self.device_of, self.sems = me, size, device_of, sems

    def on(self, step):
        return lax.rem(self.me + step, self.size)

    def back(self, step):
        return lax.rem(self.me + self.size - step, self.size)

    def copy(self, src, dst, stage, step, to):
        send_sems, recv_sems = self.sems
        return pltpu.make_async_remote_copy(
            src_ref=src,
            dst_ref=dst,
            send_sem=send_sems.at[stage, step],
            recv_sem=recv_sems.at[stage, step],
            device_id=self.device_of(to),
            device_id_type=MESH,
        )

    def steps(self):
        return range(1, self.size)

    def start_gather(self, buf, stage):
        mine = buf.at[self.me]
        for step in self.steps():
            self.copy(mine, mine, stage, step, self.on(step)).start()

    def wait_gather(self, buf, stage):
        for step in self.steps():
            theirs = buf.at[self.back(step)]
            self.copy(theirs, theirs, stage, step, self.back(step)).wait_recv()

    def end_gather(self, buf, stage):
        mine = buf.at[self.me]
        for step in self.steps():
            self.copy(mine, mine, stage, step, self.on(step)).wait_send()

    def start_scatter(self, parts, slots, stage):
        for step in self.steps():
            to = self.on(step)
            self.copy(parts.at[to], slots.at[step], stage, step, to).start()

    def wait_scatter(self, parts, slots, stage):
        for step in self.steps():
            to = self.on(step)
            self.copy(parts.at[to], slots.at[step], stage, step, to).wait()


def as_column(row):
    size = row.shape[1]
    shape = (size, size)
    same = lax.broadcasted_iota(jnp.int32, shape, 0) == lax.broadcasted_iota(jnp.int32, shape, 1)
    return jnp.sum(jnp.where(same, row, 0.0), axis=1, keepdims=True)


def as_row(column):
    size = column.shape[0]
    shape = (size, size)
    same = lax.broadcasted_iota(jnp.int32, shape, 0) == lax.broadcasted_iota(jnp.int32, shape, 1)
    return jnp.sum(jnp.where(same, column, 0.0), axis=0, keepdims=True)


def merge(stats):
    highest = jnp.max(stats[:, 0:1, :], axis=0)
    total = jnp.sum(stats[:, 1:2, :] * jnp.exp(stats[:, 0:1, :] - highest[None]), axis=0)
    return highest + jnp.log(total)


def flat_half(blocks):
    count, rows, width = blocks.shape
    return blocks.astype(jnp.float32).reshape(count * rows, width).astype(jnp.bfloat16)


def kernel(
    inner_count,
    line_count,
    pair_count,
    scale_ref,
    image_ref,
    text_ref,
    loss_ref,
    image_grad_ref,
    text_grad_ref,
    images,
    texts,
    row_stats,
    col_stats,
    row_sums,
    col_sums,
    image_parts,
    text_parts,
    image_slots,
    text_slots,
    line_send,
    line_recv,
    plane_send,
    plane_recv,
):
    inner, blk = lax.axis_index("inner"), lax.axis_index("blk")
    place, side = blk // pair_count, lax.rem(blk, pair_count)
    line = Group(
        place, line_count, lambda z: (inner, z * pair_count + side), (line_send, line_recv)
    )
    plane = Group(
        inner * pair_count + side,
        inner_count * pair_count,
        lambda g: (g // pair_count, place * pair_count + lax.rem(g, pair_count)),
        (plane_send, plane_recv),
    )
    groups = (plane, line)
    barrier = pltpu.get_barrier_semaphore()
    for group in groups:
        for step in group.steps():
            pl.semaphore_signal(
                barrier, inc=1, device_id=group.device_of(group.on(step)), device_id_type=MESH
            )

    factor = scale_ref[0]
    image_unit, image_inverse = unit_rows(image_ref[...])
    text_unit, text_inverse = unit_rows(text_ref[...])
    image_half = image_unit.astype(jnp.bfloat16)
    text_half = text_unit.astype(jnp.bfloat16)
    images[line.me] = image_half
    texts[plane.me] = text_half
    pl.semaphore_wait(barrier, plane.size + line.size - 2)
    plane.start_gather(texts, 0)
    line.start_gather(images, 0)
    image_back = image_half.astype(jnp.float32)
    text_back = text_half.astype(jnp.float32)
    diagonal = factor * jnp.sum(image_back * text_back)
    plane.wait_gather(texts, 0)
    line.wait_gather(images, 0)

    image_group = flat_half(images[...])
    text_group = flat_half(texts[...])
    image_count, text_count = image_group.shape[0], text_group.shape[0]
    logits = factor * lax.dot_general(
        image_group, text_group, (((1,), (1,)), ((), ())), preferred_element_type=jnp.float32
    )
    row_peak = jnp.max(logits, axis=1, keepdims=True)
    row_total = jnp.sum(jnp.exp(logits - row_peak), axis=1, keepdims=True)
    col_peak = jnp.max(logits, axis=0, keepdims=True)
    col_total = jnp.sum(jnp.exp(logits - col_peak), axis=0, keepdims=True)
    row_stats[line.me, 0:1, :] = as_row(row_peak)
    row_stats[line.me, 1:2, :] = as_row(row_total)
    col_stats[plane.me, 0:1, :] = col_peak
    col_stats[plane.me, 1:2, :] = col_total
    col_stats[plane.me, 2:3, :] = jnp.full((1, text_count), diagonal, jnp.float32)
    line.start_gather(row_stats, 1)
    plane.start_gather(col_stats, 1)
    line.wait_gather(row_stats, 1)
    plane.wait_gather(col_stats, 1)
    row_lse = merge(row_stats[...])
    col_lse = merge(col_stats[...])

    weights = (
        0.5 * factor * (jnp.exp(logits - as_column(row_lse)) + jnp.exp(logits - col_lse))
    ).astype(jnp.bfloat16)
    text_parts[...] = lax.dot_general(
        weights, image_group, (((0,), (0,)), ((), ())), preferred_element_type=jnp.float32
    ).reshape(text_parts.shape)
    plane.start_scatter(text_parts, text_slots, 2)
    image_parts[...] = jnp.dot(
        weights, text_group, preferred_element_type=jnp.float32
    ).reshape(image_parts.shape)
    line.start_scatter(image_parts, image_slots, 2)

    tile = row_sums.shape[1:]
    plane_diagonal = jnp.sum(col_stats[:, 2, 0:1])
    row_sums[plane.me] = jnp.full(tile, jnp.sum(row_lse), jnp.float32)
    col_sums[line.me] = jnp.full(tile, jnp.sum(col_lse) - 2.0 * plane_diagonal, jnp.float32)
    plane.start_gather(row_sums, 3)
    line.start_gather(col_sums, 3)

    plane.wait_scatter(text_parts, text_slots, 2)
    text_sum = text_parts[plane.me]
    for step in plane.steps():
        text_sum = text_sum + text_slots[step]
    text_grad_ref[...] = project(text_sum - factor * image_back, text_unit, text_inverse)
    line.wait_scatter(image_parts, image_slots, 2)
    image_sum = image_parts[line.me]
    for step in line.steps():
        image_sum = image_sum + image_slots[step]
    image_grad_ref[...] = project(image_sum - factor * text_back, image_unit, image_inverse)

    plane.wait_gather(row_sums, 3)
    line.wait_gather(col_sums, 3)
    examples = 2.0 * line.size * plane.size * image_ref.shape[0]
    whole = jnp.sum(row_sums[...], axis=0)[0, 0] + jnp.sum(col_sums[...], axis=0)[0, 0]
    loss_ref[0] = whole / examples
    for buf_line, buf_plane, stage in (
        (images, texts, 0),
        (row_stats, col_stats, 1),
        (col_sums, row_sums, 3),
    ):
        line.end_gather(buf_line, stage)
        plane.end_gather(buf_plane, stage)


def solution(mesh):
    inner_count, blk_count = mesh.shape["inner"], mesh.shape["blk"]
    pair_count = 2 if blk_count % 2 == 0 else 1
    line_count = blk_count // pair_count
    plane_count = inner_count * pair_count

    def on_device(image_emb, text_emb, logit_scale):
        rows, width = image_emb.shape
        vmem = pl.BlockSpec(memory_space=pltpu.VMEM)
        smem = pl.BlockSpec(memory_space=pltpu.SMEM)
        grad = jax.ShapeDtypeStruct((rows, width), jnp.float32)
        return pl.pallas_call(
            functools.partial(kernel, inner_count, line_count, pair_count),
            out_shape=(jax.ShapeDtypeStruct((1,), jnp.float32), grad, grad),
            in_specs=[smem, vmem, vmem],
            out_specs=(smem, vmem, vmem),
            scratch_shapes=[
                pltpu.VMEM((line_count, rows, width), jnp.bfloat16),
                pltpu.VMEM((plane_count, rows, width), jnp.bfloat16),
                pltpu.VMEM((line_count, 8, line_count * rows), jnp.float32),
                pltpu.VMEM((plane_count, 8, plane_count * rows), jnp.float32),
                pltpu.VMEM((plane_count, 8, 128), jnp.float32),
                pltpu.VMEM((line_count, 8, 128), jnp.float32),
                pltpu.VMEM((line_count, rows, width), jnp.float32),
                pltpu.VMEM((plane_count, rows, width), jnp.float32),
                pltpu.VMEM((line_count, rows, width), jnp.float32),
                pltpu.VMEM((plane_count, rows, width), jnp.float32),
                pltpu.SemaphoreType.DMA((4, line_count)),
                pltpu.SemaphoreType.DMA((4, line_count)),
                pltpu.SemaphoreType.DMA((4, plane_count)),
                pltpu.SemaphoreType.DMA((4, plane_count)),
            ],
            compiler_params=pltpu.CompilerParams(
                collective_id=0, has_side_effects=True, vmem_limit_bytes=56 * 1024 * 1024
            ),
            name="contrastive",
        )(logit_scale, image_emb, text_emb)

    in_specs = (P(("inner", "blk"), None), P(("inner", "blk"), None), P())
    out_specs = (P(), P(("inner", "blk"), None), P(("inner", "blk"), None))
    return jax.shard_map(
        on_device, mesh=mesh, in_specs=in_specs, out_specs=out_specs, check_vma=False
    )
```

time: 188 us -> 31.6 us (0.17)
  blocking collectives: 107 us -> 0 us
  waiting for transfers between devices: 54.4 us -> 0 us
  Pallas kernels: 0 us -> 26.2 us
  between operations: 17.8 us -> 3.04 us
  other arithmetic: 4.15 us -> 0 us
  matrix products: 2.46 us -> 0 us
  local copies, waits for them, and re-layouts: 0.02 us -> 2.19 us
    psum x3 -> x0, blocking collectives: 60.2 us -> none  [the longest x1 37.8 us: on_device(): lax.psum(share, ('inner', 'blk')) / (2.0 * whole_count)]
    reduce_scatter x1 -> x0, waiting for transfers between devices: 33.8 us -> none  [reduce_rows(): lax.psum_scatter(partial_value, 'blk', scatter_dimension=0, tiled=True)]
    pallas_call x0 -> x1, Pallas kernels: none -> 26.2 us  [on_device(): pl.pallas_call(functools.partial(kernel, inner_count, line_count, pair_co...]
    all_gather x2 -> x0, blocking collectives: 24.7 us -> none  [the longest x1 16.1 us: gather_rows(): return lax.all_gather(values, 'blk', axis=0, tiled=True)]
    pmax x2 -> x0, blocking collectives: 22.5 us -> none  [the longest x1 13.6 us: merge_stats(): highest = lax.pmax(peaks, 'blk')]
    unnamed x3 -> x0, waiting for transfers between devices: 20.6 us -> none
    reduce_sum x5 -> x0, other arithmetic: 3.18 us -> none  [the longest x1 1.2 us: project(): jnp.sum(gradient * direction, axis=1, keepdims=True)]
    dot_general x3 -> x0, matrix products: 2.46 us -> none  [the longest x1 1.16 us: second_pass(): lax.dot_general(weights, image_group, contract_first, preferred_element_t...]
  transfers between devices with their start and end apart: 2 -> 0, of which waited for: 2 -> 0; matrix products, arithmetic and copies ran while one was open for 1% -> 0% of each run, Pallas kernels for 0% -> 0%
where the time goes in v1:
time: 31.6 us; the launch traced here: 31.4 us
  Pallas kernels  26.2 us (83%)
  between operations  3.04 us (10%)
  local copies, waits for them, and re-layouts  2.19 us (7%)
    pallas_call x1, Pallas kernels, on_device(): pl.pallas_call(functools.partial(kernel, inner_count, line_count, pair_co...  26.2 us
    unnamed x4, local copies, waits for them, and re-layouts  2.19 us

profile of v1, /device:TPU:0, one launch (start us, length us, event | category | flops | bytes accessed | tf_op | source)
XLA Modules:
  0.0 31.4 jit_solution(17854041413729040182)
XLA Ops:
  1.3 26.2 %contrastive.1 = (f32[1]{0:T(128)}, f32[24,768]{1,0:T(8,128)}, f32[24,768]{1,0:T(8,128)}) custom-call(f32[1]{0:T(128)S(6)} %copy.9.scale_ref, f32[24,768]{1,0:T(8,128)} %image_ref.1, f32[24,768]{1,0:T(8,128)} %text_ref.1), custom_call_target="tpu_custom_call" | custom-call | tf_op jit(solution)/shard_map/contrastive/pallas_call | solution.py:235
  28.1 0.0 copy-start
  28.1 1.6 %copy.11 = f32[24,768]{1,0:T(8,128)} copy(f32[24,768]{1,0:T(8,128)} %get-tuple-element.7) | data formatting | bytes 147456
  29.6 0.0 copy-done
  29.6 0.6 %copy.12 = f32[24,768]{1,0:T(8,128)} copy(f32[24,768]{1,0:T(8,128)S(1)} %copy-done) | data formatting | bytes 147456
Async XLA Ops:
  28.1 1.6 %copy-start = (f32[24,768]{1,0:T(8,128)S(1)}, f32[24,768]{1,0:T(8,128)}, u32[]{:S(2)}) copy-start(f32[24,768]{1,0:T(8,128)} %get-tuple-element.8) | copy-start | bytes 221188

commit v2 on v1

--- a/solution.py
+++ b/solution.py
@@ -115,6 +115,8 @@
     text_parts,
     image_slots,
     text_slots,
+    image_own,
+    text_own,
     line_send,
     line_recv,
     plane_send,
@@ -180,13 +182,15 @@
     weights = (
         0.5 * factor * (jnp.exp(logits - as_column(row_lse)) + jnp.exp(logits - col_lse))
     ).astype(jnp.bfloat16)
-    text_parts[...] = lax.dot_general(
+    text_own[...] = lax.dot_general(
         weights, image_group, (((0,), (0,)), ((), ())), preferred_element_type=jnp.float32
     ).reshape(text_parts.shape)
+    text_parts[...] = text_own[...].astype(jnp.bfloat16)
     plane.start_scatter(text_parts, text_slots, 2)
-    image_parts[...] = jnp.dot(
+    image_own[...] = jnp.dot(
         weights, text_group, preferred_element_type=jnp.float32
     ).reshape(image_parts.shape)
+    image_parts[...] = image_own[...].astype(jnp.bfloat16)
     line.start_scatter(image_parts, image_slots, 2)
 
     tile = row_sums.shape[1:]
@@ -197,14 +201,14 @@
     line.start_gather(col_sums, 3)
 
     plane.wait_scatter(text_parts, text_slots, 2)
-    text_sum = text_parts[plane.me]
+    text_sum = text_own[plane.me]
     for step in plane.steps():
-        text_sum = text_sum + text_slots[step]
+        text_sum = text_sum + text_slots[step].astype(jnp.float32)
     text_grad_ref[...] = project(text_sum - factor * image_back, text_unit, text_inverse)
     line.wait_scatter(image_parts, image_slots, 2)
-    image_sum = image_parts[line.me]
+    image_sum = image_own[line.me]
     for step in line.steps():
-        image_sum = image_sum + image_slots[step]
+        image_sum = image_sum + image_slots[step].astype(jnp.float32)
     image_grad_ref[...] = project(image_sum - factor * text_back, image_unit, image_inverse)
 
     plane.wait_gather(row_sums, 3)
@@ -244,8 +248,10 @@
                 pltpu.VMEM((plane_count, 8, plane_count * rows), jnp.float32),
                 pltpu.VMEM((plane_count, 8, 128), jnp.float32),
                 pltpu.VMEM((line_count, 8, 128), jnp.float32),
-                pltpu.VMEM((line_count, rows, width), jnp.float32),
-                pltpu.VMEM((plane_count, rows, width), jnp.float32),
+                pltpu.VMEM((line_count, rows, width), jnp.bfloat16),
+                pltpu.VMEM((plane_count, rows, width), jnp.bfloat16),
+                pltpu.VMEM((line_count, rows, width), jnp.bfloat16),
+                pltpu.VMEM((plane_count, rows, width), jnp.bfloat16),
                 pltpu.VMEM((line_count, rows, width), jnp.float32),
                 pltpu.VMEM((plane_count, rows, width), jnp.float32),
                 pltpu.SemaphoreType.DMA((4, line_count)),

time: 31.6 us -> 28.6 us (0.905)
  Pallas kernels: 26.2 us -> 23.1 us
    pallas_call x1, Pallas kernels: 26.2 us -> 23.1 us  [on_device(): pl.pallas_call(functools.partial(kernel, inner_count, line_count, pair_co...]
where the time goes in v2:
time: 28.6 us; the launch traced here: 28.4 us
  Pallas kernels  23.1 us (81%)
  between operations  3.04 us (11%)
  local copies, waits for them, and re-layouts  2.19 us (8%)
    pallas_call x1, Pallas kernels, on_device(): pl.pallas_call(functools.partial(kernel, inner_count, line_count, pair_co...  23.1 us
    unnamed x4, local copies, waits for them, and re-layouts  2.19 us

profile of v2, /device:TPU:0, one launch (start us, length us, event | category | flops | bytes accessed | tf_op | source)
XLA Modules:
  0.0 28.4 jit_solution(15201417269136004598)
XLA Ops:
  1.3 23.1 %contrastive.1 = (f32[1]{0:T(128)}, f32[24,768]{1,0:T(8,128)}, f32[24,768]{1,0:T(8,128)}) custom-call(f32[1]{0:T(128)S(6)} %copy.9.scale_ref, f32[24,768]{1,0:T(8,128)} %image_ref.1, f32[24,768]{1,0:T(8,128)} %text_ref.1), custom_call_target="tpu_custom_call" | custom-call | tf_op jit(solution)/shard_map/contrastive/pallas_call | solution.py:239
  25.0 0.0 copy-start
  25.1 1.6 %copy.11 = f32[24,768]{1,0:T(8,128)} copy(f32[24,768]{1,0:T(8,128)} %get-tuple-element.7) | data formatting | bytes 147456
  26.6 0.0 copy-done
  26.6 0.6 %copy.12 = f32[24,768]{1,0:T(8,128)} copy(f32[24,768]{1,0:T(8,128)S(1)} %copy-done) | data formatting | bytes 147456
Async XLA Ops:
  25.0 1.6 %copy-start = (f32[24,768]{1,0:T(8,128)S(1)}, f32[24,768]{1,0:T(8,128)}, u32[]{:S(2)}) copy-start(f32[24,768]{1,0:T(8,128)} %get-tuple-element.8) | copy-start | bytes 221188

commit v3 on v2

--- a/solution.py
+++ b/solution.py
@@ -100,8 +100,8 @@
     line_count,
     pair_count,
     scale_ref,
-    image_ref,
-    text_ref,
+    image_hbm,
+    text_hbm,
     loss_ref,
     image_grad_ref,
     text_grad_ref,
@@ -117,11 +117,18 @@
     text_slots,
     image_own,
     text_own,
+    image_ref,
+    text_ref,
+    input_sems,
     line_send,
     line_recv,
     plane_send,
     plane_recv,
 ):
+    text_in = pltpu.make_async_copy(text_hbm, text_ref, input_sems.at[0])
+    image_in = pltpu.make_async_copy(image_hbm, image_ref, input_sems.at[1])
+    text_in.start()
+    image_in.start()
     inner, blk = lax.axis_index("inner"), lax.axis_index("blk")
     place, side = blk // pair_count, lax.rem(blk, pair_count)
     line = Group(
@@ -142,12 +149,14 @@
             )
 
     factor = scale_ref[0]
+    text_in.wait()
+    text_unit, text_inverse = unit_rows(text_ref[...])
+    text_half = text_unit.astype(jnp.bfloat16)
+    texts[plane.me] = text_half
+    image_in.wait()
     image_unit, image_inverse = unit_rows(image_ref[...])
-    text_unit, text_inverse = unit_rows(text_ref[...])
     image_half = image_unit.astype(jnp.bfloat16)
-    text_half = text_unit.astype(jnp.bfloat16)
     images[line.me] = image_half
-    texts[plane.me] = text_half
     pl.semaphore_wait(barrier, plane.size + line.size - 2)
     plane.start_gather(texts, 0)
     line.start_gather(images, 0)
@@ -179,6 +188,13 @@
     row_lse = merge(row_stats[...])
     col_lse = merge(col_stats[...])
 
+    tile = row_sums.shape[1:]
+    plane_diagonal = jnp.sum(col_stats[:, 2, 0:1])
+    row_sums[plane.me] = jnp.full(tile, jnp.sum(row_lse), jnp.float32)
+    col_sums[line.me] = jnp.full(tile, jnp.sum(col_lse) - 2.0 * plane_diagonal, jnp.float32)
+    plane.start_gather(row_sums, 3)
+    line.start_gather(col_sums, 3)
+
     weights = (
         0.5 * factor * (jnp.exp(logits - as_column(row_lse)) + jnp.exp(logits - col_lse))
     ).astype(jnp.bfloat16)
@@ -193,13 +209,6 @@
     image_parts[...] = image_own[...].astype(jnp.bfloat16)
     line.start_scatter(image_parts, image_slots, 2)
 
-    tile = row_sums.shape[1:]
-    plane_diagonal = jnp.sum(col_stats[:, 2, 0:1])
-    row_sums[plane.me] = jnp.full(tile, jnp.sum(row_lse), jnp.float32)
-    col_sums[line.me] = jnp.full(tile, jnp.sum(col_lse) - 2.0 * plane_diagonal, jnp.float32)
-    plane.start_gather(row_sums, 3)
-    line.start_gather(col_sums, 3)
-
     plane.wait_scatter(text_parts, text_slots, 2)
     text_sum = text_own[plane.me]
     for step in plane.steps():
@@ -234,26 +243,30 @@
     def on_device(image_emb, text_emb, logit_scale):
         rows, width = image_emb.shape
         vmem = pl.BlockSpec(memory_space=pltpu.VMEM)
+        hbm = pl.BlockSpec(memory_space=pl.ANY)
         smem = pl.BlockSpec(memory_space=pltpu.SMEM)
-        grad = jax.ShapeDtypeStruct((rows, width), jnp.float32)
+        near = pltpu.VMEM((rows, width), jnp.float32)
         return pl.pallas_call(
             functools.partial(kernel, inner_count, line_count, pair_count),
-            out_shape=(jax.ShapeDtypeStruct((1,), jnp.float32), grad, grad),
-            in_specs=[smem, vmem, vmem],
+            out_shape=(jax.ShapeDtypeStruct((1,), jnp.float32), near, near),
+            in_specs=[smem, hbm, hbm],
             out_specs=(smem, vmem, vmem),
             scratch_shapes=[
                 pltpu.VMEM((line_count, rows, width), jnp.bfloat16),
                 pltpu.VMEM((plane_count, rows, width), jnp.bfloat16),
-                pltpu.VMEM((line_count, 8, line_count * rows), jnp.float32),
-                pltpu.VMEM((plane_count, 8, plane_count * rows), jnp.float32),
-                pltpu.VMEM((plane_count, 8, 128), jnp.float32),
-                pltpu.VMEM((line_count, 8, 128), jnp.float32),
+                pltpu.VMEM((line_count, 2, line_count * rows), jnp.float32),
+                pltpu.VMEM((plane_count, 4, plane_count * rows), jnp.float32),
+                pltpu.VMEM((plane_count, 1, 128), jnp.float32),
+                pltpu.VMEM((line_count, 1, 128), jnp.float32),
                 pltpu.VMEM((line_count, rows, width), jnp.bfloat16),
                 pltpu.VMEM((plane_count, rows, width), jnp.bfloat16),
                 pltpu.VMEM((line_count, rows, width), jnp.bfloat16),
                 pltpu.VMEM((plane_count, rows, width), jnp.bfloat16),
                 pltpu.VMEM((line_count, rows, width), jnp.float32),
                 pltpu.VMEM((plane_count, rows, width), jnp.float32),
+                pltpu.VMEM((rows, width), jnp.float32),
+                pltpu.VMEM((rows, width), jnp.float32),
+                pltpu.SemaphoreType.DMA((2,)),
                 pltpu.SemaphoreType.DMA((4, line_count)),
                 pltpu.SemaphoreType.DMA((4, line_count)),
                 pltpu.SemaphoreType.DMA((4, plane_count)),

time: 28.6 us -> 25.5 us (0.89)
  Pallas kernels: 23.1 us -> 21.1 us
  local copies, waits for them, and re-layouts: 2.19 us -> 1.27 us
    pallas_call x1, Pallas kernels: 23.1 us -> 21.1 us  [on_device(): pl.pallas_call(functools.partial(kernel, inner_count, line_count, pair_co...]
    unnamed x4 -> x2, local copies, waits for them, and re-layouts: 2.19 us -> 1.27 us
where the time goes in v3:
time: 25.5 us; the launch traced here: 25.4 us
  Pallas kernels  21.1 us (83%)
  between operations  2.97 us (12%)
  local copies, waits for them, and re-layouts  1.27 us (5%)
    pallas_call x1, Pallas kernels, on_device(): pl.pallas_call(functools.partial(kernel, inner_count, line_count, pair_co...  21.1 us
    unnamed x2, local copies, waits for them, and re-layouts  1.27 us

profile of v3, /device:TPU:0, one launch (start us, length us, event | category | flops | bytes accessed | tf_op | source)
XLA Modules:
  0.0 25.4 jit_solution(8656097070184726545)
XLA Ops:
  1.3 21.1 %contrastive.1 = (f32[1]{0:T(128)}, f32[24,768]{1,0:T(8,128)S(1)}, f32[24,768]{1,0:T(8,128)S(1)}) custom-call(f32[1]{0:T(128)S(6)} %copy.11.scale_ref, f32[24,768]{1,0:T(8,128)} %image_hbm.1, f32[24,768]{1,0:T(8,128)} %text_hbm.1), custom_call_target="tpu_custom_call" | custom-call | tf_op jit(solution)/shard_map/contrastive/pallas_call | solution.py:249
  22.4 0.6 %copy.9 = f32[24,768]{1,0:T(8,128)} copy(f32[24,768]{1,0:T(8,128)S(1)} %get-tuple-element.4) | data formatting | bytes 147456
  23.0 0.6 %copy.10 = f32[24,768]{1,0:T(8,128)} copy(f32[24,768]{1,0:T(8,128)S(1)} %get-tuple-element.5) | data formatting | bytes 147456

commit v4 on v3

--- a/solution.py
+++ b/solution.py
@@ -158,8 +158,8 @@
     image_half = image_unit.astype(jnp.bfloat16)
     images[line.me] = image_half
     pl.semaphore_wait(barrier, plane.size + line.size - 2)
+    line.start_gather(images, 0)
     plane.start_gather(texts, 0)
-    line.start_gather(images, 0)
     image_back = image_half.astype(jnp.float32)
     text_back = text_half.astype(jnp.float32)
     diagonal = factor * jnp.sum(image_back * text_back)
@@ -198,16 +198,16 @@
     weights = (
         0.5 * factor * (jnp.exp(logits - as_column(row_lse)) + jnp.exp(logits - col_lse))
     ).astype(jnp.bfloat16)
+    image_own[...] = jnp.dot(
+        weights, text_group, preferred_element_type=jnp.float32
+    ).reshape(image_parts.shape)
+    image_parts[...] = image_own[...].astype(jnp.bfloat16)
+    line.start_scatter(image_parts, image_slots, 2)
     text_own[...] = lax.dot_general(
         weights, image_group, (((0,), (0,)), ((), ())), preferred_element_type=jnp.float32
     ).reshape(text_parts.shape)
     text_parts[...] = text_own[...].astype(jnp.bfloat16)
     plane.start_scatter(text_parts, text_slots, 2)
-    image_own[...] = jnp.dot(
-        weights, text_group, preferred_element_type=jnp.float32
-    ).reshape(image_parts.shape)
-    image_parts[...] = image_own[...].astype(jnp.bfloat16)
-    line.start_scatter(image_parts, image_slots, 2)
 
     plane.wait_scatter(text_parts, text_slots, 2)
     text_sum = text_own[plane.me]

time: 25.5 us -> 25.4 us (level)
  no operation moved by 1% of the time
where the time goes in v4:
time: 25.4 us; the launch traced here: 25.2 us
  Pallas kernels  21 us (83%)
  between operations  2.97 us (12%)
  local copies, waits for them, and re-layouts  1.27 us (5%)
    pallas_call x1, Pallas kernels, on_device(): pl.pallas_call(functools.partial(kernel, inner_count, line_count, pair_co...  21 us
    unnamed x2, local copies, waits for them, and re-layouts  1.27 us

profile of v4, /device:TPU:0, one launch (start us, length us, event | category | flops | bytes accessed | tf_op | source)
XLA Modules:
  0.0 25.2 jit_solution(6924934027049376624)
XLA Ops:
  1.3 21.0 %contrastive.1 = (f32[1]{0:T(128)}, f32[24,768]{1,0:T(8,128)S(1)}, f32[24,768]{1,0:T(8,128)S(1)}) custom-call(f32[1]{0:T(128)S(6)} %copy.11.scale_ref, f32[24,768]{1,0:T(8,128)} %image_hbm.1, f32[24,768]{1,0:T(8,128)} %text_hbm.1), custom_call_target="tpu_custom_call" | custom-call | tf_op jit(solution)/shard_map/contrastive/pallas_call | solution.py:249
  22.3 0.6 %copy.9 = f32[24,768]{1,0:T(8,128)} copy(f32[24,768]{1,0:T(8,128)S(1)} %get-tuple-element.4) | data formatting | bytes 147456
  22.9 0.6 %copy.10 = f32[24,768]{1,0:T(8,128)} copy(f32[24,768]{1,0:T(8,128)S(1)} %get-tuple-element.5) | data formatting | bytes 147456
